TPU v7x, 32 devices: a whole 2x2x4 slice. The times are simulated.
32 devices in a mesh: replica: 4 (over y, x), shard: 8 (over z, core).
Axes of the slice: x: 2, y: 2, z: 4, core: 2. Of those that a mesh axis runs over, the one named last changes fastest.
Arguments:
- block_input: float32 [32, 224, 768], P(('replica', 'shard')), may hold values from -6 to 6
- out_cotangent: float32 [32, 224, 768], P(('replica', 'shard')), may hold values from -6 to 6
- ln1_gain: bfloat16 [768], P('shard'), may hold values from 0.5 to 1.5
- ln1_bias: bfloat16 [768], P('shard'), may hold values from -3 to 3
- attn_query: bfloat16 [768, 768], P('shard'), as said below
- query_bias: bfloat16 [768], P('shard'), may hold values from -3 to 3
- attn_key: bfloat16 [768, 768], P('shard'), may hold values from -0.21875 to 0.21875
- attn_value: bfloat16 [768, 768], P('shard'), may hold values from -0.21875 to 0.21875
- value_bias: bfloat16 [768], P('shard'), may hold values from -3 to 3
- attn_out: bfloat16 [768, 768], P('shard'), may hold values from -2 to 2
- out_bias: bfloat16 [768], P('shard'), may hold values from -3 to 3
- ln2_gain: bfloat16 [768], P('shard'), may hold values from 0.5 to 1.5
- ln2_bias: bfloat16 [768], P('shard'), may hold values from -3 to 3
- fc1_weight: bfloat16 [768, 3072], P('shard'), may hold values from -0.21875 to 0.21875
- fc1_bias: bfloat16 [3072], P('shard'), may hold values from -3 to 3
- fc2_weight: bfloat16 [3072, 768], P('shard'), may hold values from -0.21875 to 0.21875
- fc2_bias: bfloat16 [768], P('shard'), may hold values from -3 to 3
Outputs:
- block_output: float32 [32, 224, 768], P(('replica', 'shard'))
- input_grad: float32 [32, 224, 768], P(('replica', 'shard'))
- ln1_gain_grad: float32 [768], P('shard')
- ln1_bias_grad: float32 [768], P('shard')
- query_grad: float32 [768, 768], P('shard')
- query_bias_grad: float32 [768], P('shard')
- key_grad: float32 [768, 768], P('shard')
- value_grad: float32 [768, 768], P('shard')
- value_bias_grad: float32 [768], P('shard')
- out_grad: float32 [768, 768], P('shard')
- out_bias_grad: float32 [768], P('shard')
- ln2_gain_grad: float32 [768], P('shard')
- ln2_bias_grad: float32 [768], P('shard')
- fc1_grad: float32 [768, 3072], P('shard')
- fc1_bias_grad: float32 [3072], P('shard')
- fc2_grad: float32 [3072, 768], P('shard')
- fc2_bias_grad: float32 [768], P('shard')
Inputs may be any that keep to these rules, and one draw needn't show every extreme that they name: `attn_query`: weights of the query projection.
All inputs are finite; a program needn't handle non-finite values.
Results may differ from a plain program's by a relative error of at most 0.014.
The roundings to bfloat16 on the way count: a program that leaves them out, or rounds other values in their place, can miss the bound.
Values may be sent and summed in bfloat16 or wider, within the bound.
A program may use at most 128 MiB of HBM per device.

v0:
```python
import jax
import jax.numpy as jnp
from jax import lax
from jax.sharding import PartitionSpec as P

HEADS = 12
HEAD_DIM = 64


def matmul(spec, left, right):
    return jnp.einsum(spec, left, right, preferred_element_type=jnp.float32)


def normalize(inputs, gain, shift):
    center = inputs - jnp.mean(inputs, axis=-1, keepdims=True)
    inv_std = lax.rsqrt(jnp.mean(center * center, axis=-1, keepdims=True) + 1e-05)
    normed = center * inv_std
    act = (normed * gain.astype(jnp.float32) + shift.astype(jnp.float32)).astype(jnp.bfloat16)
    return (normed, inv_std, act)


def norm_back(grad_out, normed, inv_std, gain):
    scaled = grad_out * gain.astype(jnp.float32)
    return inv_std * (
        scaled
        - jnp.mean(scaled, axis=-1, keepdims=True)
        - normed * jnp.mean(scaled * normed, axis=-1, keepdims=True)
    )


def gelu_parts(pre):
    cdf = 0.5 * (1.0 + jax.scipy.special.erf(pre * 0.7071067811865476))
    dens = jnp.exp(-0.5 * pre * pre) * 0.3989422804014327
    return (pre * cdf, cdf + pre * dens)


def forward_pass(block_input, attn_full, mlp_full):
    (
        ln1_gain,
        ln1_bias,
        attn_query,
        query_bias,
        attn_key,
        attn_value,
        value_bias,
        attn_out,
        out_bias,
    ) = attn_full
    ln2_gain, ln2_bias, fc1_weight, fc1_bias, fc2_weight, fc2_bias = mlp_full
    f32 = jnp.float32
    bf16 = jnp.bfloat16
    clips, frames, width = block_input.shape
    scale = HEAD_DIM ** (-0.5)
    heads_shape = (clips, frames, HEADS, HEAD_DIM)
    normed1, inv1, act1 = normalize(block_input, ln1_gain, ln1_bias)
    query = (
        ((matmul("cld,de->cle", act1, attn_query) + query_bias.astype(f32)) * scale)
        .astype(bf16)
        .reshape(heads_shape)
    )
    keys = matmul("cld,de->cle", act1, attn_key).astype(bf16).reshape(heads_shape)
    values = (
        (matmul("cld,de->cle", act1, attn_value) + value_bias.astype(f32))
        .astype(bf16)
        .reshape(heads_shape)
    )
    scores = matmul("clhe,cmhe->chlm", query, keys)
    top = jnp.max(scores, axis=-1, keepdims=True)
    log_total = top + jnp.log(jnp.sum(jnp.exp(scores - top), axis=-1, keepdims=True))
    probs = jnp.exp(scores - log_total)
    mixed = (
        matmul("chlm,cmhe->clhe", probs.astype(bf16), values)
        .astype(bf16)
        .reshape(clips, frames, width)
    )
    middle = block_input + matmul("cld,de->cle", mixed, attn_out) + out_bias.astype(f32)
    normed2, inv2, act2 = normalize(middle, ln2_gain, ln2_bias)
    pre = matmul("cld,df->clf", act2, fc1_weight) + fc1_bias.astype(f32)
    activ, slope = gelu_parts(pre)
    activ_b = activ.astype(bf16)
    block_output = middle + matmul("clf,fd->cld", activ_b, fc2_weight) + fc2_bias.astype(f32)
    saved = (
        normed1,
        inv1,
        act1,
        query,
        keys,
        values,
        log_total,
        mixed,
        normed2,
        inv2,
        act2,
        slope,
        activ_b,
    )
    return (block_output, saved)


def backward_pass(out_cotangent, saved, attn_full, mlp_full):
    (
        ln1_gain,
        ln1_bias,
        attn_query,
        query_bias,
        attn_key,
        attn_value,
        value_bias,
        attn_out,
        out_bias,
    ) = attn_full
    ln2_gain, ln2_bias, fc1_weight, fc1_bias, fc2_weight, fc2_bias = mlp_full
    (
        normed1,
        inv1,
        act1,
        query,
        keys,
        values,
        log_total,
        mixed,
        normed2,
        inv2,
        act2,
        slope,
        activ_b,
    ) = saved
    bf16 = jnp.bfloat16
    clips, frames, width = out_cotangent.shape
    scale = HEAD_DIM ** (-0.5)
    heads_shape = (clips, frames, HEADS, HEAD_DIM)
    grad_b = out_cotangent.astype(bf16)
    fc2_grad = matmul("clf,cld->fd", activ_b, grad_b)
    fc2_bias_grad = jnp.sum(out_cotangent, axis=(0, 1))
    grad_pre = matmul("cld,fd->clf", grad_b, fc2_weight) * slope
    grad_pre_b = grad_pre.astype(bf16)
    fc1_grad = matmul("cld,clf->df", act2, grad_pre_b)
    fc1_bias_grad = jnp.sum(grad_pre, axis=(0, 1))
    grad_act2 = matmul("clf,df->cld", grad_pre_b, fc1_weight)
    ln2_gain_grad = jnp.sum(grad_act2 * normed2, axis=(0, 1))
    ln2_bias_grad = jnp.sum(grad_act2, axis=(0, 1))
    grad_middle = out_cotangent + norm_back(grad_act2, normed2, inv2, ln2_gain)
    grad_mid_b = grad_middle.astype(bf16)
    out_grad = matmul("cld,cle->de", mixed, grad_mid_b)
    out_bias_grad = jnp.sum(grad_middle, axis=(0, 1))
    grad_mixed = matmul("cle,de->cld", grad_mid_b, attn_out).astype(bf16).reshape(heads_shape)
    again = jnp.exp(matmul("clhe,cmhe->chlm", query, keys) - log_total)
    grad_probs = matmul("clhe,cmhe->chlm", grad_mixed, values)
    inner = jnp.sum(again * grad_probs, axis=-1, keepdims=True)
    grad_scores = (again * (grad_probs - inner)).astype(bf16)
    grad_query = matmul("chlm,cmhe->clhe", grad_scores, keys).reshape(clips, frames, width) * scale
    grad_keys = matmul("chlm,clhe->cmhe", grad_scores, query).reshape(clips, frames, width)
    grad_values = matmul("chlm,clhe->cmhe", again.astype(bf16), grad_mixed).reshape(
        clips, frames, width
    )
    query_bias_grad = jnp.sum(grad_query, axis=(0, 1))
    value_bias_grad = jnp.sum(grad_values, axis=(0, 1))
    grad_query_b = grad_query.astype(bf16)
    grad_keys_b = grad_keys.astype(bf16)
    grad_values_b = grad_values.astype(bf16)
    query_grad = matmul("cld,cle->de", act1, grad_query_b)
    key_grad = matmul("cld,cle->de", act1, grad_keys_b)
    value_grad = matmul("cld,cle->de", act1, grad_values_b)
    grad_act1 = (
        matmul("cle,de->cld", grad_query_b, attn_query)
        + matmul("cle,de->cld", grad_keys_b, attn_key)
        + matmul("cle,de->cld", grad_values_b, attn_value)
    )
    ln1_gain_grad = jnp.sum(grad_act1 * normed1, axis=(0, 1))
    ln1_bias_grad = jnp.sum(grad_act1, axis=(0, 1))
    input_grad = grad_middle + norm_back(grad_act1, normed1, inv1, ln1_gain)
    attn_grads = (
        ln1_gain_grad,
        ln1_bias_grad,
        query_grad,
        query_bias_grad,
        key_grad,
        value_grad,
        value_bias_grad,
        out_grad,
        out_bias_grad,
    )
    mlp_grads = (ln2_gain_grad, ln2_bias_grad, fc1_grad, fc1_bias_grad, fc2_grad, fc2_bias_grad)
    return (input_grad, attn_grads, mlp_grads)


def body(
    block_input,
    out_cotangent,
    ln1_gain,
    ln1_bias,
    attn_query,
    query_bias,
    attn_key,
    attn_value,
    value_bias,
    attn_out,
    out_bias,
    ln2_gain,
    ln2_bias,
    fc1_weight,
    fc1_bias,
    fc2_weight,
    fc2_bias,
):
    attn_full = (
        lax.all_gather(ln1_gain, "shard", axis=0, tiled=True),
        lax.all_gather(ln1_bias, "shard", axis=0, tiled=True),
        lax.all_gather(attn_query, "shard", axis=0, tiled=True),
        lax.all_gather(query_bias, "shard", axis=0, tiled=True),
        lax.all_gather(attn_key, "shard", axis=0, tiled=True),
        lax.all_gather(attn_value, "shard", axis=0, tiled=True),
        lax.all_gather(value_bias, "shard", axis=0, tiled=True),
        lax.all_gather(attn_out, "shard", axis=0, tiled=True),
        lax.all_gather(out_bias, "shard", axis=0, tiled=True),
    )
    mlp_full = (
        lax.all_gather(ln2_gain, "shard", axis=0, tiled=True),
        lax.all_gather(ln2_bias, "shard", axis=0, tiled=True),
        lax.all_gather(fc1_weight, "shard", axis=0, tiled=True),
        lax.all_gather(fc1_bias, "shard", axis=0, tiled=True),
        lax.all_gather(fc2_weight, "shard", axis=0, tiled=True),
        lax.all_gather(fc2_bias, "shard", axis=0, tiled=True),
    )
    block_output, saved = forward_pass(block_input, attn_full, mlp_full)
    attn_back = (
        lax.all_gather(ln1_gain, "shard", axis=0, tiled=True),
        lax.all_gather(ln1_bias, "shard", axis=0, tiled=True),
        lax.all_gather(attn_query, "shard", axis=0, tiled=True),
        lax.all_gather(query_bias, "shard", axis=0, tiled=True),
        lax.all_gather(attn_key, "shard", axis=0, tiled=True),
        lax.all_gather(attn_value, "shard", axis=0, tiled=True),
        lax.all_gather(value_bias, "shard", axis=0, tiled=True),
        lax.all_gather(attn_out, "shard", axis=0, tiled=True),
        lax.all_gather(out_bias, "shard", axis=0, tiled=True),
    )
    mlp_back = (
        lax.all_gather(ln2_gain, "shard", axis=0, tiled=True),
        lax.all_gather(ln2_bias, "shard", axis=0, tiled=True),
        lax.all_gather(fc1_weight, "shard", axis=0, tiled=True),
        lax.all_gather(fc1_bias, "shard", axis=0, tiled=True),
        lax.all_gather(fc2_weight, "shard", axis=0, tiled=True),
        lax.all_gather(fc2_bias, "shard", axis=0, tiled=True),
    )
    input_grad, attn_grads, mlp_grads = backward_pass(out_cotangent, saved, attn_back, mlp_back)
    mlp_owned = (
        lax.psum_scatter(mlp_grads[0], "shard", scatter_dimension=0, tiled=True),
        lax.psum_scatter(mlp_grads[1], "shard", scatter_dimension=0, tiled=True),
        lax.psum_scatter(mlp_grads[2], "shard", scatter_dimension=0, tiled=True),
        lax.psum_scatter(mlp_grads[3], "shard", scatter_dimension=0, tiled=True),
        lax.psum_scatter(mlp_grads[4], "shard", scatter_dimension=0, tiled=True),
        lax.psum_scatter(mlp_grads[5], "shard", scatter_dimension=0, tiled=True),
    )
    attn_owned = (
        lax.psum_scatter(attn_grads[0], "shard", scatter_dimension=0, tiled=True),
        lax.psum_scatter(attn_grads[1], "shard", scatter_dimension=0, tiled=True),
        lax.psum_scatter(attn_grads[2], "shard", scatter_dimension=0, tiled=True),
        lax.psum_scatter(attn_grads[3], "shard", scatter_dimension=0, tiled=True),
        lax.psum_scatter(attn_grads[4], "shard", scatter_dimension=0, tiled=True),
        lax.psum_scatter(attn_grads[5], "shard", scatter_dimension=0, tiled=True),
        lax.psum_scatter(attn_grads[6], "shard", scatter_dimension=0, tiled=True),
        lax.psum_scatter(attn_grads[7], "shard", scatter_dimension=0, tiled=True),
        lax.psum_scatter(attn_grads[8], "shard", scatter_dimension=0, tiled=True),
    )
    totals = lax.psum(
        (
            attn_owned[0],
            attn_owned[1],
            attn_owned[2],
            attn_owned[3],
            attn_owned[4],
            attn_owned[5],
            attn_owned[6],
            attn_owned[7],
            attn_owned[8],
            mlp_owned[0],
            mlp_owned[1],
            mlp_owned[2],
            mlp_owned[3],
            mlp_owned[4],
            mlp_owned[5],
        ),
        "replica",
    )
    return (
        block_output,
        input_grad,
        totals[0],
        totals[1],
        totals[2],
        totals[3],
        totals[4],
        totals[5],
        totals[6],
        totals[7],
        totals[8],
        totals[9],
        totals[10],
        totals[11],
        totals[12],
        totals[13],
        totals[14],
    )


def solution(mesh):
    placed = (
        P(("replica", "shard"), None, None),
        P(("replica", "shard"), None, None),
        P("shard"),
        P("shard"),
        P("shard", None),
        P("shard"),
        P("shard", None),
        P("shard", None),
        P("shard"),
        P("shard", None),
        P("shard"),
        P("shard"),
        P("shard"),
        P("shard", None),
        P("shard"),
        P("shard", None),
        P("shard"),
    )
    return jax.shard_map(
        body,
        mesh=mesh,
        in_specs=placed,
        out_specs=(
            P(("replica", "shard"), None, None),
            P(("replica", "shard"), None, None),
            P("shard"),
            P("shard"),
            P("shard", None),
            P("shard"),
            P("shard", None),
            P("shard", None),
            P("shard"),
            P("shard", None),
            P("shard"),
            P("shard"),
            P("shard"),
            P("shard", None),
            P("shard"),
            P("shard", None),
            P("shard"),
        ),
        check_vma=False,
    )
```

profile of v0, /device:TPU:0, one launch (start us, length us, event | category | flops | bytes accessed | tf_op | source)
XLA Modules:
  0.0 693.2 jit_solution(3192558629059282865)
XLA Ops:
  19.9 30.7 %all-reduce.20 = (bf16[768]{0:T(1024)(128)(2,1)S(1)}, bf16[768]{0:T(1024)(128)(2,1)S(1)}, bf16[768]{0:T(1024)(128)(2,1)S(1)}, bf16[768]{0:T(1024)(128)(2,1)S(1)}...) all-reduce(bf16[768]{0:T(1024)(128)(2,1)S(1)} %dynamic-update-slice, ...), channel_id=1, replica_groups=mesh['replica'=4,'shard'=8] {'shard'}, use_global_device_ids=true, to_apply=%add.1 | all-reduce | flops 6144 | bytes 24576
  51.3 12.9 %all-gather = bf16[8,1,384]{2,1,0:T(2,128)(2,1)S(1)} all-gather(bf16[1,1,384]{2,1,0:T(2,128)(2,1)S(1)} %reshape.379), channel_id=1, replica_groups=mesh['replica'=4,'shard'=8] {'shard'}, dimensions={0}, use_global_device_ids=true | all-gather | bytes 6912 | tf_op jit(solution)/shard_map/all_gather | solution.py:221
  71.4 12.3 %all-gather.12.cloned.1.call-done = bf16[768,768]{1,0:T(8,128)(2,1)} async-done(((bf16[96,768]{1,0:T(8,128)(2,1)}), bf16[768,768]{1,0:T(8,128)(2,1)}) %all-gather.12.cloned.1.call-update) | async-done | bytes 1179664 | tf_op jit(solution)/shard_map/all_gather | solution.py:211
  89.9 17.8 %all-gather.14.cloned.1.call-done = bf16[768,768]{1,0:T(8,128)(2,1)} async-done(((bf16[96,768]{1,0:T(8,128)(2,1)}), bf16[768,768]{1,0:T(8,128)(2,1)}) %all-gather.14.cloned.1.call-update) | async-done | bytes 1179664 | tf_op jit(solution)/shard_map/all_gather | solution.py:214
  107.6 1.9 fusion.47
  110.7 49.3 %all-gather.16.cloned.1.call-done = bf16[768,3072]{1,0:T(8,128)(2,1)} async-done(((bf16[96,3072]{1,0:T(8,128)(2,1)}), bf16[768,3072]{1,0:T(8,128)(2,1)}) %all-gather.16.cloned.1.call-update) | async-done | bytes 4718608 | tf_op jit(solution)/shard_map/all_gather | solution.py:220
  160.0 5.5 convolution_add_fusion
  165.4 46.0 %all-gather.18.cloned.1.call-done = bf16[3072,768]{1,0:T(8,128)(2,1)} async-done(((bf16[384,768]{1,0:T(8,128)(2,1)}), bf16[3072,768]{1,0:T(8,128)(2,1)}) %all-gather.18.cloned.1.call-update) | async-done | bytes 4718608 | tf_op jit(solution)/shard_map/all_gather | solution.py:222
  211.5 5.4 fusion.48
  230.1 2.0 convolution_convert_fusion
  232.8 3.0 fusion.51
  243.8 5.2 fusion.20
  250.1 7.1 %fusion.31 = f32[3072,768]{1,0:T(8,128)} fusion(f32[1,224,768]{2,1,0:T(8,128)S(1)} %copy-done.20, f32[224,3072]{1,0:T(8,128)} %convolution_add_fusion), kind=kOutput, calls=%fused_computation.66 | convolution fusion | flops 1060577280 | bytes 12877824 | tf_op jit(solution)/shard_map/clf,cld->fd/dot_general | solution.py:11
  257.4 8.6 %reduce-scatter.7.cloned.1.call-done = f32[96,768]{1,0:T(8,128)} async-done(((f32[768,768]{1,0:T(8,128)}), f32[96,768]{1,0:T(8,128)}) %reduce-scatter.7.cloned.1.call-update) | async-done | bytes 294928 | tf_op jit(solution)/shard_map/reduce_scatter | solution.py:257
  266.0 38.3 %reduce-scatter.9.cloned.1.call-done = f32[96,768]{1,0:T(8,128)} async-done(((f32[768,768]{1,0:T(8,128)}), f32[96,768]{1,0:T(8,128)}) %reduce-scatter.9.cloned.1.call-update) | async-done | bytes 294928 | tf_op jit(solution)/shard_map/reduce_scatter | solution.py:259
  304.3 38.3 %reduce-scatter.11.cloned.1.call-done = f32[96,768]{1,0:T(8,128)} async-done(((f32[768,768]{1,0:T(8,128)}), f32[96,768]{1,0:T(8,128)}) %reduce-scatter.11.cloned.1.call-update) | async-done | bytes 294928 | tf_op jit(solution)/shard_map/reduce_scatter | solution.py:260
  342.6 38.2 %reduce-scatter.13.cloned.1.call-done = f32[96,768]{1,0:T(8,128)} async-done(((f32[768,768]{1,0:T(8,128)}), f32[96,768]{1,0:T(8,128)}) %reduce-scatter.13.cloned.1.call-update) | async-done | bytes 294928 | tf_op jit(solution)/shard_map/reduce_scatter | solution.py:262
  380.8 100.6 %reduce-scatter.15.cloned.1.call-done = f32[96,3072]{1,0:T(8,128)} async-done(((f32[768,3072]{1,0:T(8,128)}), f32[96,3072]{1,0:T(8,128)}) %reduce-scatter.15.cloned.1.call-update) | async-done | bytes 1179664 | tf_op jit(solution)/shard_map/reduce_scatter | solution.py:249
  481.4 100.1 %reduce-scatter.17.cloned.1.call-done = f32[384,768]{1,0:T(8,128)} async-done(((f32[3072,768]{1,0:T(8,128)}), f32[384,768]{1,0:T(8,128)}) %reduce-scatter.17.cloned.1.call-update) | async-done | bytes 1179664 | tf_op jit(solution)/shard_map/reduce_scatter | solution.py:251
  584.3 2.1 fusion.49
  588.9 26.5 %all-reduce.17 = (f32[768]{0:T(1024)S(1)}, f32[768]{0:T(1024)S(1)}, f32[768]{0:T(1024)S(1)}, f32[768]{0:T(1024)S(1)}, f32[768]{0:T(1024)S(1)}, /*index=5*/f32[76...) all-reduce(f32[768]{0:T(1024)S(1)} %get-tuple-element.19, ...), channel_id=2, replica_groups=mesh['replica'=4,'shard'=8] {'shard'}, use_global_device_ids=true, to_apply=%region_12.0.clone | all-reduce | flops 9216 | bytes 73728
  616.0 11.4 %all-reduce.18 = (f32[96]{0:T(128)}, f32[96]{0:T(128)}, f32[96]{0:T(128)}, f32[96]{0:T(128)}, f32[96]{0:T(128)}, /*index=5*/f32[96]{0:T(128)}, f32[96]{0:T(128)}, f32[384]{0:T(512)}, f32[96]{0:T(128)}) all-reduce(f32[96]{0:T(128)S(1)} %dynamic-slice.9, f32[96]{0:T(128)S(1)} %dynamic-slice.11, ...), channel_id=1, replica_groups=mesh['replica'=4,'shard'=8] {'replica'}, use_global_device_ids=true, to_apply=%region_13.0 | all-reduce | flops 1152 | bytes 9216 | tf_op jit(solution)/shard_map/psum | solution.py:265
  629.5 4.7 fusion.9
  634.2 43.5 %all-reduce.23.cloned.1.call-done = (f32[96,768]{1,0:T(8,128)}, f32[96,768]{1,0:T(8,128)}, f32[96,768]{1,0:T(8,128)}, f32[96,768]{1,0:T(8,128)}, f32[96,3072]{1,0:T(8,128)}, /*index=5*/f32[384,768]{1,0:T(8,128)}) async-done(((f32[96,768]{1,0:T(8,128)}, f32[96,768]{1,0:T(8,128)}, f32[96,768]{1,0:T(8,128)}, f32[96,768]{1,0:T(8,128)}, f32[96,3072]{1,0:T(8,128)}, /*index=5*/f32[384,768]{1,0:T(8,128)}), ...) | async-done | bytes 3538960 | tf_op jit(solution)/shard_map/psum | solution.py:265
  (164 shorter events, 65.4 us)
Async XLA Ops:
  7.2 58.4 %copy-start = (f32[1,224,768]{2,1,0:T(8,128)S(1)}, f32[1,224,768]{2,1,0:T(8,128)}, u32[]{:S(2)}) copy-start(f32[1,224,768]{2,1,0:T(8,128)} %param.17) | copy-start | bytes 2064388
  7.2 58.8 %all-gather.8.cloned.1.call-start = ((), (), s32[]{:S(2)}) async-start(), calls=%async_computation.6 | async-start | bytes 1327104 | tf_op jit(solution)/shard_map/all_gather | solution.py:212
  7.9 60.8 %all-gather.10.cloned.1.call-start = ((), (), s32[]{:S(2)}) async-start(), calls=%async_computation.7 | async-start | bytes 1327104 | tf_op jit(solution)/shard_map/all_gather | solution.py:209
  8.7 75.0 %all-gather.12.cloned.1.call-start = ((), (), s32[]{:S(2)}) async-start(), calls=%async_computation.8 | async-start | bytes 1327104 | tf_op jit(solution)/shard_map/all_gather | solution.py:211
  9.4 98.2 %all-gather.14.cloned.1.call-start = ((), (), s32[]{:S(2)}) async-start(), calls=%async_computation.9 | async-start | bytes 1327104 | tf_op jit(solution)/shard_map/all_gather | solution.py:214
  10.0 150.0 %all-gather.16.cloned.1.call-start = ((), (), s32[]{:S(2)}) async-start(), calls=%async_computation.10 | async-start | bytes 5308416 | tf_op jit(solution)/shard_map/all_gather | solution.py:220
  10.6 200.9 %all-gather.18.cloned.1.call-start = ((), (), s32[]{:S(2)}) async-start(), calls=%async_computation.11 | async-start | bytes 5308416 | tf_op jit(solution)/shard_map/all_gather | solution.py:222
  11.2 254.8 %reduce-scatter.7.cloned.1.call-start = ((), (), s32[]{:S(2)}) async-start(), calls=%async_computation.12 | async-start | bytes 2654208 | tf_op jit(solution)/shard_map/reduce_scatter | solution.py:257
  66.0 19.4 %copy-start.7 = (bf16[224,768]{1,0:T(8,128)(2,1)}, bf16[224,768]{1,0:T(8,128)(2,1)S(1)}, u32[]{:S(2)}) copy-start(bf16[224,768]{1,0:T(8,128)(2,1)S(1)} %fusion.26) | copy-start | bytes 1032196
  211.5 5.4 copy-start.5
  211.5 5.4 copy-start.26
  230.0 74.3 %reduce-scatter.9.cloned.1.call-start = ((), (), s32[]{:S(2)}) async-start(), calls=%async_computation.13 | async-start | bytes 2654208 | tf_op jit(solution)/shard_map/reduce_scatter | solution.py:259
  235.9 106.7 %reduce-scatter.11.cloned.1.call-start = ((), (), s32[]{:S(2)}) async-start(), calls=%async_computation.14 | async-start | bytes 2654208 | tf_op jit(solution)/shard_map/reduce_scatter | solution.py:260
  237.8 2.8 copy-start.3
  237.8 2.8 copy-start.18
  240.5 140.2 %reduce-scatter.13.cloned.1.call-start = ((), (), s32[]{:S(2)}) async-start(), calls=%async_computation.15 | async-start | bytes 2654208 | tf_op jit(solution)/shard_map/reduce_scatter | solution.py:262
  242.5 238.9 %reduce-scatter.15.cloned.1.call-start = ((), (), s32[]{:S(2)}) async-start(), calls=%async_computation.16 | async-start | bytes 10616832 | tf_op jit(solution)/shard_map/reduce_scatter | solution.py:249
  249.0 332.4 %reduce-scatter.17.cloned.1.call-start = ((), (), s32[]{:S(2)}) async-start(), calls=%async_computation.17 | async-start | bytes 10616832 | tf_op jit(solution)/shard_map/reduce_scatter | solution.py:251
  257.3 420.4 %all-reduce.23.cloned.1.call-start = ((), (), s32[]{:S(2)}) async-start(), calls=%async_computation.18 | async-start | bytes 7077888 | tf_op jit(solution)/shard_map/psum | solution.py:265
  581.5 4.9 copy-start.11
  584.3 3.6 copy-start.16
  584.3 3.6 copy-start.25
  677.7 6.9 copy-start.24
  677.7 7.9 %copy-start.23 = (f32[384,768]{1,0:T(8,128)S(1)}, f32[384,768]{1,0:T(8,128)}, u32[]{:S(2)}) copy-start(f32[384,768]{1,0:T(8,128)} %get-tuple-element.97) | copy-start | bytes 3538948
  (16 other events, 23.6 us)
Sparse Core Ops, SparseCore 0:
  9.6 25.5 all-gather.7
  36.9 22.6 all-gather.9
  61.3 22.3 all-gather.11
  85.2 22.4 all-gather.13
  109.1 50.8 all-gather.15
  161.5 49.9 all-gather.17
  230.1 35.7 reduce-scatter.6
  268.3 35.9 reduce-scatter.8
  306.6 35.9 reduce-scatter.10
  344.8 35.9 reduce-scatter.12
  383.1 98.2 reduce-scatter.14
  483.6 97.8 reduce-scatter.16
  585.3 92.3 all-reduce.22
where the time goes:
time: 694 us; the launch traced here: 693 us
  waiting for transfers between devices  497 us (72%)
  blocking collectives  81.5 us (12%)
  matrix products  61.1 us (9%)
  local copies, waits for them, and re-layouts  30.7 us (4%)
  between operations  16.4 us (2%)
    reduce_scatter x1, waiting for transfers between devices, body(): lax.psum_scatter(mlp_grads[2], 'shard', scatter_dimension=0, tiled=True)  101 us
    reduce_scatter x1, waiting for transfers between devices, body(): lax.psum_scatter(mlp_grads[4], 'shard', scatter_dimension=0, tiled=True)  100 us
    dot_general x24, matrix products, matmul(): return jnp.einsum(spec, left, right, preferred_element_type=jnp.float32)  61.1 us
    unnamed x2, blocking collectives  57.2 us
    all_gather x1, waiting for transfers between devices, body(): lax.all_gather(fc1_weight, 'shard', axis=0, tiled=True)  49.3 us
    all_gather x1, waiting for transfers between devices, body(): lax.all_gather(fc2_weight, 'shard', axis=0, tiled=True)  46 us
    psum x1, waiting for transfers between devices, body(): lax.psum((attn_owned[0], attn_owned[1], attn_owned[2], attn_owned[3], att...  43.5 us
    reduce_scatter x1, waiting for transfers between devices, body(): lax.psum_scatter(attn_grads[4], 'shard', scatter_dimension=0, tiled=True)  38.3 us
  transfers between devices with their start and end apart: 13, of which 11 were waited for; matrix products, arithmetic and copies ran while one was open for 9% of the time, Pallas kernels for 0%

commit v1 on v0

v1 whole, which is shorter than its diff:
```python
import jax
import jax.numpy as jnp
from jax import lax
from jax.sharding import PartitionSpec as P

HEADS = 12
HEAD_DIM = 64


def matmul(spec, left, right):
    return jnp.einsum(spec, left, right, preferred_element_type=jnp.float32)


def normalize(inputs, gain, shift):
    center = inputs - jnp.mean(inputs, axis=-1, keepdims=True)
    inv_std = lax.rsqrt(jnp.mean(center * center, axis=-1, keepdims=True) + 1e-05)
    normed = center * inv_std
    act = (normed * gain.astype(jnp.float32) + shift.astype(jnp.float32)).astype(jnp.bfloat16)
    return (normed, inv_std, act)


def norm_back(grad_out, normed, inv_std, gain):
    scaled = grad_out * gain.astype(jnp.float32)
    return inv_std * (
        scaled
        - jnp.mean(scaled, axis=-1, keepdims=True)
        - normed * jnp.mean(scaled * normed, axis=-1, keepdims=True)
    )


def gelu_parts(pre):
    cdf = 0.5 * (1.0 + jax.scipy.special.erf(pre * 0.7071067811865476))
    dens = jnp.exp(-0.5 * pre * pre) * 0.3989422804014327
    return (pre * cdf, cdf + pre * dens)


def forward_pass(block_input, attn_full, mlp_full):
    ln1_gain, ln1_bias, attn_qkv, query_bias, value_bias, attn_out, out_bias = attn_full
    ln2_gain, ln2_bias, fc1_weight, fc1_bias, fc2_weight, fc2_bias = mlp_full
    f32 = jnp.float32
    bf16 = jnp.bfloat16
    clips, frames, width = block_input.shape
    scale = HEAD_DIM ** (-0.5)
    heads_shape = (clips, frames, HEADS, HEAD_DIM)
    normed1, inv1, act1 = normalize(block_input, ln1_gain, ln1_bias)
    mixed_in = matmul("cld,de->cle", act1, attn_qkv)
    query = ((mixed_in[..., :width] + query_bias.astype(f32)) * scale).astype(bf16)
    keys = mixed_in[..., width : 2 * width].astype(bf16)
    values = (mixed_in[..., 2 * width :] + value_bias.astype(f32)).astype(bf16)
    query, keys, values = (part.reshape(heads_shape) for part in (query, keys, values))
    scores = matmul("clhe,cmhe->chlm", query, keys)
    top = jnp.max(scores, axis=-1, keepdims=True)
    log_total = top + jnp.log(jnp.sum(jnp.exp(scores - top), axis=-1, keepdims=True))
    probs = jnp.exp(scores - log_total)
    mixed = (
        matmul("chlm,cmhe->clhe", probs.astype(bf16), values)
        .astype(bf16)
        .reshape(clips, frames, width)
    )
    middle = block_input + matmul("cld,de->cle", mixed, attn_out) + out_bias.astype(f32)
    normed2, inv2, act2 = normalize(middle, ln2_gain, ln2_bias)
    pre = matmul("cld,df->clf", act2, fc1_weight) + fc1_bias.astype(f32)
    activ, slope = gelu_parts(pre)
    activ_b = activ.astype(bf16)
    block_output = middle + matmul("clf,fd->cld", activ_b, fc2_weight) + fc2_bias.astype(f32)
    saved = (
        normed1,
        inv1,
        act1,
        query,
        keys,
        values,
        log_total,
        mixed,
        normed2,
        inv2,
        act2,
        slope,
        activ_b,
    )
    return (block_output, saved)


def backward_pass(out_cotangent, saved, attn_full, mlp_full):
    ln1_gain, ln1_bias, attn_qkv, query_bias, value_bias, attn_out, out_bias = attn_full
    ln2_gain, ln2_bias, fc1_weight, fc1_bias, fc2_weight, fc2_bias = mlp_full
    (
        normed1,
        inv1,
        act1,
        query,
        keys,
        values,
        log_total,
        mixed,
        normed2,
        inv2,
        act2,
        slope,
        activ_b,
    ) = saved
    bf16 = jnp.bfloat16
    clips, frames, width = out_cotangent.shape
    scale = HEAD_DIM ** (-0.5)
    heads_shape = (clips, frames, HEADS, HEAD_DIM)
    grad_b = out_cotangent.astype(bf16)
    fc2_grad = matmul("clf,cld->fd", activ_b, grad_b)
    fc2_bias_grad = jnp.sum(out_cotangent, axis=(0, 1))
    grad_pre = matmul("cld,fd->clf", grad_b, fc2_weight) * slope
    grad_pre_b = grad_pre.astype(bf16)
    fc1_grad = matmul("cld,clf->df", act2, grad_pre_b)
    fc1_bias_grad = jnp.sum(grad_pre, axis=(0, 1))
    grad_act2 = matmul("clf,df->cld", grad_pre_b, fc1_weight)
    ln2_gain_grad = jnp.sum(grad_act2 * normed2, axis=(0, 1))
    ln2_bias_grad = jnp.sum(grad_act2, axis=(0, 1))
    grad_middle = out_cotangent + norm_back(grad_act2, normed2, inv2, ln2_gain)
    grad_mid_b = grad_middle.astype(bf16)
    out_grad = matmul("cld,cle->de", mixed, grad_mid_b)
    out_bias_grad = jnp.sum(grad_middle, axis=(0, 1))
    grad_mixed = matmul("cle,de->cld", grad_mid_b, attn_out).astype(bf16).reshape(heads_shape)
    again = jnp.exp(matmul("clhe,cmhe->chlm", query, keys) - log_total)
    grad_probs = matmul("clhe,cmhe->chlm", grad_mixed, values)
    inner = jnp.sum(again * grad_probs, axis=-1, keepdims=True)
    grad_scores = (again * (grad_probs - inner)).astype(bf16)
    grad_query = matmul("chlm,cmhe->clhe", grad_scores, keys).reshape(clips, frames, width) * scale
    grad_keys = matmul("chlm,clhe->cmhe", grad_scores, query).reshape(clips, frames, width)
    grad_values = matmul("chlm,clhe->cmhe", again.astype(bf16), grad_mixed).reshape(
        clips, frames, width
    )
    query_bias_grad = jnp.sum(grad_query, axis=(0, 1))
    value_bias_grad = jnp.sum(grad_values, axis=(0, 1))
    grad_query_b = grad_query.astype(bf16)
    grad_keys_b = grad_keys.astype(bf16)
    grad_values_b = grad_values.astype(bf16)
    joined = jnp.concatenate((grad_query_b, grad_keys_b, grad_values_b), axis=-1)
    qkv_grad = matmul("cld,cle->de", act1, joined)
    grad_act1 = matmul("cle,de->cld", joined, attn_qkv)
    ln1_gain_grad = jnp.sum(grad_act1 * normed1, axis=(0, 1))
    ln1_bias_grad = jnp.sum(grad_act1, axis=(0, 1))
    input_grad = grad_middle + norm_back(grad_act1, normed1, inv1, ln1_gain)
    attn_grads = (
        ln1_gain_grad,
        ln1_bias_grad,
        qkv_grad,
        query_bias_grad,
        value_bias_grad,
        out_grad,
        out_bias_grad,
    )
    mlp_grads = (ln2_gain_grad, ln2_bias_grad, fc1_grad, fc1_bias_grad, fc2_grad, fc2_bias_grad)
    return (input_grad, attn_grads, mlp_grads)


def body(
    block_input,
    out_cotangent,
    ln1_gain,
    ln1_bias,
    attn_query,
    query_bias,
    attn_key,
    attn_value,
    value_bias,
    attn_out,
    out_bias,
    ln2_gain,
    ln2_bias,
    fc1_weight,
    fc1_bias,
    fc2_weight,
    fc2_bias,
):
    f32 = jnp.float32
    bf16 = jnp.bfloat16
    rows, width = attn_query.shape
    per_row = fc1_bias.shape[0] // rows
    narrow = (
        ln1_gain,
        ln1_bias,
        query_bias,
        value_bias,
        out_bias,
        ln2_gain,
        ln2_bias,
        fc2_bias,
    )
    columns = jnp.concatenate(
        (jnp.stack(narrow, axis=1), fc1_bias.reshape(rows, per_row)), axis=1
    )
    used = columns.shape[1]
    spare = -used % 128
    packed = jnp.concatenate(
        (attn_query, attn_key, attn_value, attn_out, jnp.pad(columns, ((0, 0), (0, spare)))),
        axis=1,
    )
    attn_all = lax.all_gather(packed, "shard", axis=0, tiled=True)
    fc1_all = lax.all_gather(fc1_weight, "shard", axis=0, tiled=True)
    fc2_all = lax.all_gather(fc2_weight, "shard", axis=0, tiled=True)
    small = attn_all[:, 4 * width : 4 * width + used]
    g1, b1, bq, bv, bo, g2, b2, bf2 = (small[:, i] for i in range(len(narrow)))
    bf1 = small[:, len(narrow) :].reshape(-1)
    attn_full = (g1, b1, attn_all[:, : 3 * width], bq, bv, attn_all[:, 3 * width : 4 * width], bo)
    mlp_full = (g2, b2, fc1_all, bf1, fc2_all, bf2)
    block_output, saved = forward_pass(block_input, attn_full, mlp_full)
    input_grad, attn_grads, mlp_grads = backward_pass(out_cotangent, saved, attn_full, mlp_full)
    dg1, db1, dqkv, dbq, dbv, dout, dbo = attn_grads
    dg2, db2, dfc1, dbf1, dfc2, dbf2 = mlp_grads

    def owned(grad):
        part = lax.psum_scatter(grad.astype(bf16), "shard", scatter_dimension=0, tiled=True)
        return lax.psum(part, "replica").astype(f32)

    fc2_owned = owned(dfc2)
    fc1_owned = owned(dfc1)
    thin = jnp.concatenate(
        (
            jnp.stack((dg1, db1, dbq, dbv, dbo, dg2, db2, dbf2), axis=1),
            dbf1.reshape(-1, per_row),
        ),
        axis=1,
    )
    attn_owned = owned(
        jnp.concatenate((dqkv, dout, jnp.pad(thin, ((0, 0), (0, spare)))), axis=1)
    )
    base = 4 * width
    og1, ob1, obq, obv, obo, og2, ob2, obf2 = (
        attn_owned[:, base + i] for i in range(len(narrow))
    )
    obf1 = attn_owned[:, base + len(narrow) : base + used].reshape(-1)
    return (
        block_output,
        input_grad,
        og1,
        ob1,
        attn_owned[:, :width],
        obq,
        attn_owned[:, width : 2 * width],
        attn_owned[:, 2 * width : 3 * width],
        obv,
        attn_owned[:, 3 * width : 4 * width],
        obo,
        og2,
        ob2,
        fc1_owned,
        obf1,
        fc2_owned,
        obf2,
    )


def solution(mesh):
    placed = (
        P(("replica", "shard"), None, None),
        P(("replica", "shard"), None, None),
        P("shard"),
        P("shard"),
        P("shard", None),
        P("shard"),
        P("shard", None),
        P("shard", None),
        P("shard"),
        P("shard", None),
        P("shard"),
        P("shard"),
        P("shard"),
        P("shard", None),
        P("shard"),
        P("shard", None),
        P("shard"),
    )
    return jax.shard_map(
        body,
        mesh=mesh,
        in_specs=placed,
        out_specs=(
            P(("replica", "shard"), None, None),
            P(("replica", "shard"), None, None),
            P("shard"),
            P("shard"),
            P("shard", None),
            P("shard"),
            P("shard", None),
            P("shard", None),
            P("shard"),
            P("shard", None),
            P("shard"),
            P("shard"),
            P("shard"),
            P("shard", None),
            P("shard"),
            P("shard", None),
            P("shard"),
        ),
        check_vma=False,
    )
```

time: 694 us -> 431 us (0.62)
  waiting for transfers between devices: 497 us -> 320 us
  blocking collectives: 81.5 us -> 0 us
  matrix products: 61.1 us -> 52.4 us
  other arithmetic: 5.95 us -> 13.6 us
    reduce_scatter x6 -> x3, waiting for transfers between devices: 324 us -> 122 us  [owned(): lax.psum_scatter(grad.astype(bf16), 'shard', scatter_dimension=0, tiled=T...]
    unnamed x2 -> x0, blocking collectives: 57.2 us -> none
    unnamed x87 -> x59, local copies, waits for them, and re-layouts: 25.9 us -> 7.88 us
    psum x1, waiting for transfers between devices: 43.5 us -> 60.1 us  [owned(): return lax.psum(part, 'replica').astype(f32)]
    all_gather x1 -> x0, blocking collectives: 12.9 us -> none  [body(): lax.all_gather(fc1_bias, 'shard', axis=0, tiled=True)]
    psum x1 -> x0, blocking collectives: 11.4 us -> none  [body(): lax.psum((attn_owned[0], attn_owned[1], attn_owned[2], attn_owned[3], att...]
    all_gather x6 -> x3, waiting for transfers between devices: 125 us -> 137 us  [the longest x1 54.1 us: body(): attn_all = lax.all_gather(packed, 'shard', axis=0, tiled=True)]
    dot_general x24 -> x18, matrix products: 61.1 us -> 52.4 us  [matmul(): return jnp.einsum(spec, left, right, preferred_element_type=jnp.float32)]
  transfers between devices with their start and end apart: 13 -> 7, of which waited for: 11 -> 7; matrix products, arithmetic and copies ran while one was open for 9% -> 16% of each run, Pallas kernels for 0% -> 0%
where the time goes in v1:
time: 431 us; the launch traced here: 430 us
  waiting for transfers between devices  320 us (74%)
  matrix products  52.4 us (12%)
  local copies, waits for them, and re-layouts  29.2 us (7%)
  between operations  14.6 us (3%)
  other arithmetic  13.6 us (3%)
    reduce_scatter x3, waiting for transfers between devices, owned(): lax.psum_scatter(grad.astype(bf16), 'shard', scatter_dimension=0, tiled=T...  122 us
    psum x1, waiting for transfers between devices, owned(): return lax.psum(part, 'replica').astype(f32)  60.1 us
    all_gather x1, waiting for transfers between devices, body(): attn_all = lax.all_gather(packed, 'shard', axis=0, tiled=True)  54.1 us
    dot_general x18, matrix products, matmul(): return jnp.einsum(spec, left, right, preferred_element_type=jnp.float32)  52.4 us
    all_gather x1, waiting for transfers between devices, body(): fc2_all = lax.all_gather(fc2_weight, 'shard', axis=0, tiled=True)  45.7 us
    all_gather x1, waiting for transfers between devices, body(): fc1_all = lax.all_gather(fc1_weight, 'shard', axis=0, tiled=True)  36.8 us
  transfers between devices with their start and end apart: 7, of which 7 were waited for; matrix products, arithmetic and copies ran while one was open for 16% of the time, Pallas kernels for 0%

profile of v1, /device:TPU:0, one launch (start us, length us, event | category | flops | bytes accessed | tf_op | source)
XLA Modules:
  0.0 430.5 jit_solution(5986682349822183564)
XLA Ops:
  15.6 54.1 %all-gather.4.cloned.1.call-done = bf16[768,3200]{1,0:T(8,128)(2,1)} async-done(((bf16[96,3200]{1,0:T(8,128)(2,1)}), bf16[768,3200]{1,0:T(8,128)(2,1)}) %all-gather.4.cloned.1.call-update) | async-done | bytes 4915216 | tf_op jit(solution)/shard_map/all_gather | solution.py:196
  71.0 3.1 convert_reduce_fusion
  74.1 3.0 convolution_bitcast_fusion
  84.4 36.8 %all-gather.6.cloned.1.call-done = bf16[768,3072]{1,0:T(8,128)(2,1)} async-done(((bf16[96,3072]{1,0:T(8,128)(2,1)}), bf16[768,3072]{1,0:T(8,128)(2,1)}) %all-gather.6.cloned.1.call-update) | async-done | bytes 4718608 | tf_op jit(solution)/shard_map/all_gather | solution.py:197
  121.2 5.9 %multiply_convert_fusion.1 = (bf16[224,3072]{1,0:T(8,128)(2,1)}, f32[224,3072]{1,0:T(8,128)}) fusion(f32[3072]{0:T(1024)S(1)} %reshape.429, bf16[768,3072]{1,0:T(8,128)(2,1)} %all-gather.6.cloned.1.call-done, f32[1,224,768]{2,1,0:T(8,128)S(1)} %get-tuple-element.60, f32[768]{0:T(1024)S(1)} %get-tuple-element.18, f32[768]{0:T(1024)S(1)} %get-tuple-element.19, ...), kind=kOutput, calls=%fused_computation.19 | convolution fusion | flops 1061953536 | bytes 9555712 | tf_op jit(solution)/shard_map/cld,df->clf/dot_general | solution.py:11
  127.2 45.7 %all-gather.8.cloned.1.call-done = bf16[3072,768]{1,0:T(8,128)(2,1)} async-done(((bf16[384,768]{1,0:T(8,128)(2,1)}), bf16[3072,768]{1,0:T(8,128)(2,1)}) %all-gather.8.cloned.1.call-update) | async-done | bytes 4718608 | tf_op jit(solution)/shard_map/all_gather | solution.py:198
  172.9 5.2 %fusion.57 = (bf16[3072]{0:T(1024)(128)(2,1)S(1)}, bf16[224,3072]{1,0:T(8,128)(2,1)S(1)}) fusion(f32[224,3072]{1,0:T(8,128)} %get-tuple-element.62, bf16[3072,768]{1,0:T(8,128)(2,1)} %all-gather.8.cloned.1.call-done, f32[1,224,768]{2,1,0:T(8,128)} %param.18), kind=kOutput, calls=%fused_computation.121 | convolution fusion | flops 1064702976 | bytes 9541632 | tf_op jit(solution)/shard_map/cld,fd->clf/dot_general | solution.py:11
  179.3 3.8 convolution_convert_fusion.2
  183.2 5.1 %convolution_convert_fusion.1 = bf16[3072,768]{1,0:T(8,128)(2,1)} fusion(bf16[224,3072]{1,0:T(8,128)(2,1)} %get-tuple-element.61, f32[1,224,768]{2,1,0:T(8,128)} %param.18), kind=kOutput, calls=%fused_computation.3 | convolution fusion | flops 1059495936 | bytes 6782976 | tf_op jit(solution)/shard_map/clf,cld->fd/dot_general | solution.py:11
  189.6 4.5 %fusion.19 = (bf16[768]{0:T(1024)(128)(2,1)S(1)}, f32[224]{0:T(256)S(1)}, f32[224,768]{1,0:T(8,128)S(1)}) fusion(f32[1,224,768]{2,1,0:T(8,128)S(1)} %get-tuple-element.60, f32[224]{0:T(256)S(1)} %add_rsqrt_fusion, f32[224]{0:T(256)S(1)} %broadcast_multiply_fusion.4, f32[768]{0:T(1024)S(1)} %get-tuple-element.19, ...), kind=kOutput, calls=%fused_computation.46 | convolution fusion | flops 1058167808 | bytes 7478400 | tf_op jit(solution)/shard_map/clf,df->cld/dot_general | solution.py:11
  198.1 2.6 convolution_convert_fusion.6
  202.6 2.4 fusion.52
  211.1 2.0 convolution_convert_fusion.4
  213.2 3.7 fusion.20
  219.7 2.3 concatenate.20
  222.5 2.6 convolution_convert_fusion
  225.1 2.6 fusion.1
  227.8 9.1 %reduce-scatter.6.cloned.1.call-done = bf16[96,3072]{1,0:T(8,128)(2,1)} async-done(((bf16[768,3072]{1,0:T(8,128)(2,1)}), bf16[96,3072]{1,0:T(8,128)(2,1)}) %reduce-scatter.6.cloned.1.call-update) | async-done | bytes 589840 | tf_op jit(solution)/shard_map/reduce_scatter | solution.py:210
  236.9 55.5 %reduce-scatter.8.cloned.1.call-done = bf16[384,768]{1,0:T(8,128)(2,1)} async-done(((bf16[3072,768]{1,0:T(8,128)(2,1)}), bf16[384,768]{1,0:T(8,128)(2,1)}) %reduce-scatter.8.cloned.1.call-update) | async-done | bytes 589840 | tf_op jit(solution)/shard_map/reduce_scatter | solution.py:210
  292.5 57.4 %reduce-scatter.4.cloned.1.call-done = bf16[96,3200]{1,0:T(8,128)(2,1)} async-done(((bf16[768,3200]{1,0:T(8,128)(2,1)}), bf16[96,3200]{1,0:T(8,128)(2,1)}) %reduce-scatter.4.cloned.1.call-update) | async-done | bytes 614416 | tf_op jit(solution)/shard_map/reduce_scatter | solution.py:210
  349.9 2.2 fusion.23
  352.1 4.4 %fusion.13 = f32[1,224,768]{2,1,0:T(8,128)} fusion(f32[1,224,768]{2,1,0:T(8,128)S(1)} %get-tuple-element.60, bf16[224,3072]{1,0:T(8,128)(2,1)S(1)} %copy-done.11, bf16[3072,768]{1,0:T(8,128)(2,1)} %all-gather.8.cloned.1.call-done, f32[768]{0:T(1024)S(1)} %get-tuple-element.17), kind=kOutput, calls=%fused_computation.34 | convolution fusion | flops 1057308672 | bytes 7474176 | tf_op jit(solution)/shard_map/clf,fd->cld/dot_general | solution.py:11
  356.5 60.1 %all-reduce.5.cloned.1.call-done = (bf16[96,3200]{1,0:T(8,128)(2,1)}, bf16[96,3072]{1,0:T(8,128)(2,1)}, bf16[384,768]{1,0:T(8,128)(2,1)}) async-done(((bf16[96,3200]{1,0:T(8,128)(2,1)}, bf16[96,3072]{1,0:T(8,128)(2,1)}, bf16[384,768]{1,0:T(8,128)(2,1)}), (bf16[96,3200]{1,0:T(8,128)(2,1)}, bf16[96,3072]{1,0:T(8,128)(2,1)}, bf16[384,768]{1,0:T(8,128)(2,1)})) %all-reduce.5.cloned.1.call-update) | async-done | bytes 1794064 | tf_op jit(solution)/shard_map/psum | solution.py:211
  417.6 2.2 fusion.54
  (122 shorter events, 39.3 us)
Async XLA Ops:
  7.2 8.1 %copy-start.1 = (f32[1,224,768]{2,1,0:T(8,128)S(1)}, f32[1,224,768]{2,1,0:T(8,128)}, u32[]{:S(2)}) copy-start(f32[1,224,768]{2,1,0:T(8,128)} %param.17) | copy-start | bytes 2064388
  7.2 62.5 %all-gather.4.cloned.1.call-start = ((), (), s32[]{:S(2)}) async-start(), calls=%async_computation.3 | async-start | bytes 5529600 | tf_op jit(solution)/shard_map/all_gather | solution.py:196
  13.7 107.5 %all-gather.6.cloned.1.call-start = ((), (), s32[]{:S(2)}) async-start(), calls=%async_computation.4 | async-start | bytes 5308416 | tf_op jit(solution)/shard_map/all_gather | solution.py:197
  14.5 158.4 %all-gather.8.cloned.1.call-start = ((), (), s32[]{:S(2)}) async-start(), calls=%async_computation.5 | async-start | bytes 5308416 | tf_op jit(solution)/shard_map/all_gather | solution.py:198
  15.2 221.7 %reduce-scatter.6.cloned.1.call-start = ((), (), s32[]{:S(2)}) async-start(), calls=%async_computation.7 | async-start | bytes 5308416 | tf_op jit(solution)/shard_map/reduce_scatter | solution.py:210
  183.1 109.3 %reduce-scatter.8.cloned.1.call-start = ((), (), s32[]{:S(2)}) async-start(), calls=%async_computation.8 | async-start | bytes 5308416 | tf_op jit(solution)/shard_map/reduce_scatter | solution.py:210
  188.3 161.6 %reduce-scatter.4.cloned.1.call-start = ((), (), s32[]{:S(2)}) async-start(), calls=%async_computation.6 | async-start | bytes 5529600 | tf_op jit(solution)/shard_map/reduce_scatter | solution.py:210
  189.6 4.7 %copy-start.13 = (f32[1,224,768]{2,1,0:T(8,128)S(1)}, f32[1,224,768]{2,1,0:T(8,128)}, u32[]{:S(2)}) copy-start(f32[1,224,768]{2,1,0:T(8,128)} %param.18) | copy-start | bytes 2064388
  194.6 3.5 copy-start.4
  209.6 3.6 copy-start.3
  209.6 3.6 copy-start.24
  210.0 3.1 copy-start.25
  213.2 3.8 copy-start.26
  213.2 6.5 %copy-start.16 = (bf16[768,4]{1,0:T(8,128)(2,1)S(1)}, bf16[768,4]{1,0:T(8,128)(2,1)}, u32[]{:S(2)}) copy-start(bf16[768,4]{1,0:T(8,128)(2,1)} %reshape.420) | copy-start | bytes 18436
  213.2 6.5 %copy-start.17 = (bf16[768,1]{1,0:T(8,128)(2,1)S(1)}, bf16[768,1]{1,0:T(8,128)(2,1)}, u32[]{:S(2)}) copy-start(bf16[768,1]{1,0:T(8,128)(2,1)} %stack.76) | copy-start | bytes 4612
  213.2 6.4 %copy-start.18 = (bf16[768,1]{1,0:T(8,128)(2,1)S(1)}, bf16[768,1]{1,0:T(8,128)(2,1)}, u32[]{:S(2)}) copy-start(bf16[768,1]{1,0:T(8,128)(2,1)} %stack.78) | copy-start | bytes 4612
  213.2 6.4 %copy-start.19 = (bf16[768,1]{1,0:T(8,128)(2,1)S(1)}, bf16[768,1]{1,0:T(8,128)(2,1)}, u32[]{:S(2)}) copy-start(bf16[768,1]{1,0:T(8,128)(2,1)} %stack.77) | copy-start | bytes 4612
  213.2 6.4 %copy-start.20 = (bf16[768,1]{1,0:T(8,128)(2,1)S(1)}, bf16[768,1]{1,0:T(8,128)(2,1)}, u32[]{:S(2)}) copy-start(bf16[768,1]{1,0:T(8,128)(2,1)} %stack.79) | copy-start | bytes 4612
  217.0 5.0 %copy-start.5 = (f32[1,224,768]{2,1,0:T(8,128)S(1)}, f32[1,224,768]{2,1,0:T(8,128)}, u32[]{:S(2)}) copy-start(f32[1,224,768]{2,1,0:T(8,128)} %copy-done.4) | copy-start | bytes 2064388
  217.0 5.0 %copy-start.10 = (bf16[12,64,224]{2,1,0:T(8,128)(2,1)S(1)}, bf16[12,64,224]{2,1,0:T(8,128)(2,1)}, u32[]{:S(2)}) copy-start(bf16[12,64,224]{2,1,0:T(8,128)(2,1)} %copy-done.9) | copy-start | bytes 1032196
  227.7 124.4 %copy-start.11 = (bf16[224,3072]{1,0:T(8,128)(2,1)S(1)}, bf16[224,3072]{1,0:T(8,128)(2,1)}, u32[]{:S(2)}) copy-start(bf16[224,3072]{1,0:T(8,128)(2,1)} %get-tuple-element.61) | copy-start | bytes 4128772
  227.7 188.9 %all-reduce.5.cloned.1.call-start = ((), (), s32[]{:S(2)}) async-start(), calls=%async_computation.9 | async-start | bytes 3588096 | tf_op jit(solution)/shard_map/psum | solution.py:211
  416.7 3.9 copy-start.23
  417.6 4.1 copy-start.22
  (10 other events, 16.8 us)
Sparse Core Ops, SparseCore 0:
  13.8 55.8 all-gather.3
  71.4 49.8 all-gather.5
  122.9 49.9 all-gather.7
  183.3 53.6 reduce-scatter.5
  239.1 53.3 reduce-scatter.7
  294.6 55.1 reduce-scatter.3
  353.4 63.2 all-reduce.4
